TPU v7x, 128 devices: a whole 4x4x4 slice. The times are simulated.
128 devices in a mesh: dp: 8 (over y_lo, x), mp: 16 (over y_hi, z, core).
Axes of the slice: x: 4, y: 4 (y_hi: 2, y_lo: 2; y = y_hi * 2 + y_lo), z: 4, core: 2. Of those that a mesh axis runs over, the one named last changes fastest.
Arguments:
- tokens: bfloat16 [16384, 2304], P(('dp', 'mp')), may hold values from -6 to 6
- ada_ffn: float32 [16, 2, 2304], P('dp'), may hold values from -4 to 4
- ffn_gate: float32 [16, 2304], P('dp'), may hold values from 0.5 to 1.5
- up_weight: bfloat16 [2304, 9216], P(None, 'mp'), may hold values from -0.125 to 0.125
- up_bias: float32 [9216], P('mp'), may hold values from -6 to 6
- down_weight: bfloat16 [9216, 2304], P('mp'), may hold values from -0.125 to 0.125
- down_bias: float32 [2304], replicated, may hold values from -6 to 6
- ada_head: float32 [16, 2, 2304], P('dp'), may hold values from -4 to 4
- head_weight: bfloat16 [2304, 4096], P(None, 'mp'), may hold values from -0.125 to 0.125
- head_bias: float32 [4096], P('mp'), may hold values from -6 to 6
- gumbel_noise: float32 [8, 1024, 4096], P('dp', None, 'mp'), as said below
- codebook: bfloat16 [4096, 32], P('mp'), may hold values from -16 to 16
- phi_weight: float32 [32, 32, 3, 3], replicated, may hold values from -0.375 to 0.375
- phi_bias: float32 [32], replicated, may hold values from -6 to 6
- f_hat: float32 [8, 32, 1024], P('dp', None, 'mp'), may hold values from -6 to 6
Outputs:
- block_out: bfloat16 [16384, 2304], P(('dp', 'mp'))
- f_hat_out: float32 [8, 32, 1024], P('dp', None, 'mp')
Inputs may be any that keep to these rules, and one draw needn't show every extreme that they name: `gumbel_noise`: noise added to the guided logits.
All inputs are finite; a program needn't handle non-finite values.
Results may differ from a plain program's by a relative error of at most 0.024.
Values may be sent and summed in bfloat16 or wider, within the bound.
A program may use at most 256 MiB of HBM per device.

v0:
```python
import jax
import jax.numpy as jnp
from jax import lax
from jax.sharding import PartitionSpec as P

SIDE = 32
NEW = 1024
GUIDE = 1.5


def from_partner(value, axis, apart):
    mask = 2**apart
    pairs = [(source, source ^ mask) for source in range(lax.axis_size(axis))]
    return lax.ppermute(value, axis, pairs)


def norm_rows(values):
    row_mean = jnp.mean(values, axis=-1, keepdims=True)
    centred = values - row_mean
    spread = jnp.mean(centred * centred, axis=-1, keepdims=True)
    return centred * lax.rsqrt(spread + 1e-06)


def per_image(lookup, row_images):
    picked = jnp.broadcast_to(lookup[0], (row_images.shape[0],) + lookup.shape[1:])
    chosen = (row_images == 1).reshape((-1,) + (1,) * (lookup.ndim - 1))
    picked = jnp.where(chosen, lookup[1], picked)
    return picked


def modulate(values, ada_rows):
    return (norm_rows(values) * (1.0 + ada_rows[:, 1]) + ada_rows[:, 0]).astype(jnp.bfloat16)


def body(
    tokens,
    ada_ffn,
    ffn_gate,
    up_weight,
    up_bias,
    down_weight,
    down_bias,
    ada_head,
    head_weight,
    head_bias,
    gumbel_noise,
    codebook,
    phi_weight,
    phi_bias,
    f_hat,
):
    row_count = tokens.shape[0]
    shard_count = lax.axis_size("mp")
    mp_index = lax.axis_index("mp")
    group_rows = row_count * shard_count
    own_images = (mp_index * row_count + jnp.arange(row_count, dtype=jnp.int32)) // NEW
    gathered = lax.all_gather(tokens, "mp", axis=0, tiled=True)
    row_images = jnp.arange(group_rows, dtype=jnp.int32) // NEW
    full_hidden = jax.nn.gelu(
        jnp.dot(
            modulate(gathered.astype(jnp.float32), per_image(ada_ffn, row_images)),
            up_weight,
            preferred_element_type=jnp.float32,
        )
        + up_bias,
        approximate=True,
    ).astype(jnp.bfloat16)
    summed = lax.psum_scatter(
        jnp.dot(full_hidden, down_weight, preferred_element_type=jnp.float32),
        "mp",
        scatter_dimension=0,
        tiled=True,
    )
    block_out = (
        tokens.astype(jnp.float32) + per_image(ffn_gate, own_images) * (summed + down_bias)
    ).astype(jnp.bfloat16)
    full_out = lax.all_gather(block_out, "mp", axis=0, tiled=True)
    logits = (
        jnp.dot(
            modulate(full_out.astype(jnp.float32), per_image(ada_head, row_images)),
            head_weight,
            preferred_element_type=jnp.float32,
        )
        + head_bias
    )
    half_rows = group_rows // 2
    upper_half = lax.axis_index("dp") // (lax.axis_size("dp") // 2)
    kept_rows = lax.dynamic_slice_in_dim(logits, upper_half * half_rows, half_rows, 0)
    sent_rows = lax.dynamic_slice_in_dim(logits, (1 - upper_half) * half_rows, half_rows, 0)
    twin_rows = from_partner(sent_rows, "dp", lax.axis_size("dp").bit_length() - 2)
    cond_rows = jnp.where(upper_half == 0, kept_rows, twin_rows)
    uncond_rows = jnp.where(upper_half == 0, twin_rows, kept_rows)
    scores = (1.0 + GUIDE) * cond_rows - GUIDE * uncond_rows + gumbel_noise.reshape(half_rows, -1)
    row_peak = jnp.max(scores, axis=1)
    weights = jnp.exp(scores - row_peak[:, None]).astype(jnp.bfloat16)
    row_total = jnp.sum(weights.astype(jnp.float32), axis=1)
    mixed_code = jnp.dot(weights, codebook, preferred_element_type=jnp.float32)
    global_peak = lax.pmax(row_peak, "mp")
    factor = jnp.exp(row_peak - global_peak)
    row_total, mixed_code = (
        lax.psum((row_total * factor).astype(jnp.bfloat16), "mp").astype(jnp.float32),
        lax.psum((mixed_code * factor[:, None]).astype(jnp.bfloat16), "mp").astype(jnp.float32),
    )
    soft_code = mixed_code / row_total[:, None]
    pair_count = f_hat.shape[0]
    channels = f_hat.shape[1]
    band_rows = f_hat.shape[2] // SIDE
    code_maps = soft_code.reshape(pair_count, SIDE, SIDE, channels)
    padded = jnp.pad(code_maps, ((0, 0), (1, 1), (1, 1), (0, 0)))
    window = lax.dynamic_slice_in_dim(padded, mp_index * band_rows, band_rows + 2, 1)
    conv_out = (
        jnp.zeros((pair_count, channels, band_rows, SIDE), jnp.float32)
        + phi_bias[None, :, None, None]
    )
    for row_step in range(3):
        for col_step in range(3):
            conv_out = conv_out + jnp.einsum(
                "pyxc,oc->poyx",
                window[:, row_step : row_step + band_rows, col_step : col_step + SIDE, :],
                phi_weight[:, :, row_step, col_step],
                precision=lax.Precision.HIGHEST,
            )
    own_cells = jnp.transpose(window[:, 1 : band_rows + 1, 1 : SIDE + 1, :], (0, 3, 1, 2))
    f_hat_out = f_hat + (0.5 * own_cells + 0.5 * conv_out).reshape(
        pair_count, channels, band_rows * SIDE
    )
    return (block_out, f_hat_out)


def solution(mesh):
    in_specs = (
        P(("dp", "mp"), None),
        P("dp", None, None),
        P("dp", None),
        P(None, "mp"),
        P("mp"),
        P("mp", None),
        P(),
        P("dp", None, None),
        P(None, "mp"),
        P("mp"),
        P("dp", None, "mp"),
        P("mp", None),
        P(),
        P(),
        P("dp", None, "mp"),
    )
    out_specs = (P(("dp", "mp"), None), P("dp", None, "mp"))
    return jax.shard_map(body, mesh=mesh, in_specs=in_specs, out_specs=out_specs, check_vma=False)
```

profile of v0, /device:TPU:0, one launch (start us, length us, event | category | flops | bytes accessed | tf_op | source)
XLA Modules:
  0.0 590.4 jit_solution(9555418837395056854)
XLA Ops:
  8.8 24.7 %broadcast_select_fusion = (f32[2048,2,2304]{2,0,1:T(8,128)}, f32[2048,2,2304]{2,0,1:T(8,128)}) fusion(f32[2,2304]{1,0:T(2,128)S(1)} %get-tuple-element.9, f32[2,2304]{1,0:T(2,128)S(1)} %get-tuple-element.8, pred[2048]{0:T(1024)(128)(4,1)S(1)} %fusion.70, f32[2,2304]{1,0:T(2,128)S(1)} %get-tuple-element.14, f32[2,2304]{1,0:T(2,128)S(1)} %get-tuple-element.15), kind=kLoop, calls=%fused_computation.22 | loop fusion | flops 18874368 | bytes 75573248 | tf_op jit(solution)/shard_map/jit(_where)/select_n | solution.py:27
  33.4 57.1 %all-gather.3.cloned.1.call-done = bf16[2048,2304]{1,0:T(8,128)(2,1)} async-done(((bf16[128,2304]{1,0:T(8,128)(2,1)}), bf16[2048,2304]{1,0:T(8,128)(2,1)}) %all-gather.3.cloned.1.call-update) | async-done | bytes 9437200 | tf_op jit(solution)/shard_map/all_gather | solution.py:57
  90.6 5.1 convert_reduce_fusion.1
  95.7 1.2 copy-done.3
  96.9 2.6 fusion.8
  99.6 28.5 %fusion.29 = f32[2048,2304]{1,0:T(8,128)} fusion(bf16[576,2304]{1,0:T(8,128)(2,1)S(1)} %copy-done, bf16[2304,576]{0,1:T(8,128)(2,1)} %param.18, bf16[2048,2304]{1,0:T(8,128)(2,1)} %all-gather.3.cloned.1.call-done, f32[2048,2,2304]{2,0,1:T(8,128)} %get-tuple-element.13, f32[2048]{0:T(1024)S(1)} %add_rsqrt_fusion.1, f32[2048]{0:T(1024)S(1)} %broadcast_multiply_fusion.1, ...), kind=kOutput, calls=%fused_computation.35 | convolution fusion | flops 10916462592 | bytes 71387392 | tf_op jit(solution)/shard_map/dot_general | solution.py:69
  128.9 156.1 %reduce-scatter.2.cloned.1.call-done = f32[128,2304]{1,0:T(8,128)} async-done(((f32[2048,2304]{1,0:T(8,128)}), f32[128,2304]{1,0:T(8,128)}) %reduce-scatter.2.cloned.1.call-update) | async-done | bytes 1179664 | tf_op jit(solution)/shard_map/reduce_scatter | solution.py:68
  285.0 2.4 add_convert_fusion
  287.6 75.9 %all-gather.5.cloned.1.call-done = bf16[2048,2304]{1,0:T(8,128)(2,1)} async-done(((bf16[128,2304]{1,0:T(8,128)(2,1)}), bf16[2048,2304]{1,0:T(8,128)(2,1)}) %all-gather.5.cloned.1.call-update) | async-done | bytes 9437200 | tf_op jit(solution)/shard_map/all_gather | solution.py:77
  363.5 5.1 convert_reduce_fusion
  368.6 1.2 copy-done.2
  369.8 2.6 fusion.4
  372.5 14.0 %fusion.31 = f32[2048,256]{0,1:T(8,128)S(1)} fusion(bf16[2304,256]{1,0:T(8,128)(2,1)S(1)} %copy-done.12, bf16[2048,2304]{1,0:T(8,128)(2,1)S(1)} %copy-done.2, f32[2048,2,2304]{2,0,1:T(8,128)} %get-tuple-element.12, f32[2048]{0:T(1024)S(1)} %add_rsqrt_fusion, f32[2048]{0:T(1024)S(1)} %broadcast_multiply_fusion, f32[256]{0:T(256)S(1)} %copy-done.14), kind=kOutput, calls=%fused_computation.36 | convolution fusion | flops 2449473536 | bytes 50480128 | tf_op jit(solution)/shard_map/dot_general | solution.py:79
  386.5 1.3 copy-done.5
  387.8 1.1 constant_dynamic-slice_fusion
  389.5 2.5 copy.17
  392.0 22.5 %collective-permute-done = f32[1024,256]{0,1:T(8,128)} collective-permute-done((f32[1024,256]{0,1:T(8,128)}, f32[1024,256]{0,1:T(8,128)}, u32[]{:S(2)}, u32[]{:S(2)}) %collective-permute-start) | collective-permute-done | bytes 1048608 | tf_op jit(solution)/shard_map/ppermute | solution.py:14
  414.5 3.3 fusion.97
  417.8 33.6 %pmax.7 = f32[1024]{0:T(1024)S(1)} all-reduce(f32[1024]{0:T(1024)S(1)} %get-tuple-element.6), channel_id=1, replica_groups=mesh['dp'=8,'mp'=16] {'mp'}, use_global_device_ids=true, to_apply=%region_6.7 | all-reduce | flops 1024 | bytes 8192 | tf_op jit(solution)/shard_map/pmax | solution.py:98
  451.4 1.4 convert_reduce_fusion.2
  452.8 2.1 fusion.39
  454.9 33.2 %psum.15 = bf16[1024]{0:T(1024)(128)(2,1)S(1)} all-reduce(bf16[1024]{0:T(1024)(128)(2,1)S(1)} %get-tuple-element.4), channel_id=1, replica_groups=mesh['dp'=8,'mp'=16] {'mp'}, use_global_device_ids=true, to_apply=%region_9.10 | all-reduce | flops 1024 | bytes 4096 | tf_op jit(solution)/shard_map/psum | solution.py:101
  488.1 92.3 %all-reduce.3.cloned.1.call-done = bf16[1024,32]{0,1:T(8,128)(2,1)} async-done(((bf16[1024,32]{0,1:T(8,128)(2,1)}), bf16[1024,32]{0,1:T(8,128)(2,1)}) %all-reduce.3.cloned.1.call-update) | async-done | bytes 65552 | tf_op jit(solution)/shard_map/psum | solution.py:102
  580.4 0.9 convert_divide_fusion
  (58 shorter events, 5.7 us)
Async XLA Ops:
  7.2 92.4 %copy-start = (bf16[576,2304]{1,0:T(8,128)(2,1)S(1)}, bf16[576,2304]{1,0:T(8,128)(2,1)}, u32[]{:S(2)}) copy-start(bf16[576,2304]{1,0:T(8,128)(2,1)} %param.20) | copy-start | bytes 7962628
  7.2 83.4 %all-gather.3.cloned.1.call-start = ((), (), s32[]{:S(2)}) async-start(), calls=%async_computation.1 | async-start | bytes 10027008 | tf_op jit(solution)/shard_map/all_gather | solution.py:57
  7.9 277.0 %reduce-scatter.2.cloned.1.call-start = ((), (), s32[]{:S(2)}) async-start(), calls=%async_computation.2 | async-start | bytes 20054016 | tf_op jit(solution)/shard_map/reduce_scatter | solution.py:68
  33.4 66.1 %copy-start.13 = (f32[576]{0:T(1024)S(1)}, f32[576]{0:T(1024)}, u32[]{:S(2)}) copy-start(f32[576]{0:T(1024)} %param.19) | copy-start | bytes 6916
  90.6 6.4 %copy-start.3 = (bf16[2048,2304]{1,0:T(8,128)(2,1)S(1)}, bf16[2048,2304]{1,0:T(8,128)(2,1)}, u32[]{:S(2)}) copy-start(bf16[2048,2304]{1,0:T(8,128)(2,1)} %all-gather.3.cloned.1.call-done) | copy-start | bytes 28311556
  128.1 0.7 copy-start.7
  128.1 156.9 %copy-start.4 = (bf16[128,2304]{1,0:T(8,128)(2,1)S(1)}, bf16[128,2304]{1,0:T(8,128)(2,1)}, u32[]{:S(2)}) copy-start(bf16[128,2304]{1,0:T(8,128)(2,1)} %param.15) | copy-start | bytes 1769476
  128.1 156.9 %copy-start.10 = (f32[2304]{0:T(1024)S(1)}, f32[2304]{0:T(1024)}, u32[]{:S(2)}) copy-start(f32[2304]{0:T(1024)} %param.21) | copy-start | bytes 27652
  128.1 235.3 %all-gather.5.cloned.1.call-start = ((), (), s32[]{:S(2)}) async-start(), calls=%async_computation.3 | async-start | bytes 10027008 | tf_op jit(solution)/shard_map/all_gather | solution.py:77
  287.3 293.1 %all-reduce.3.cloned.1.call-start = ((), (), s32[]{:S(2)}) async-start(), calls=%async_computation.4 | async-start | bytes 131072 | tf_op jit(solution)/shard_map/psum | solution.py:102
  287.6 84.8 %copy-start.14 = (f32[256]{0:T(256)S(1)}, f32[256]{0:T(256)}, u32[]{:S(2)}) copy-start(f32[256]{0:T(256)} %param.24) | copy-start | bytes 3076
  363.5 6.4 %copy-start.2 = (bf16[2048,2304]{1,0:T(8,128)(2,1)S(1)}, bf16[2048,2304]{1,0:T(8,128)(2,1)}, u32[]{:S(2)}) copy-start(bf16[2048,2304]{1,0:T(8,128)(2,1)} %all-gather.5.cloned.1.call-done) | copy-start | bytes 28311556
  363.5 9.0 %copy-start.12 = (bf16[2304,256]{1,0:T(8,128)(2,1)S(1)}, bf16[2304,256]{1,0:T(8,128)(2,1)}, u32[]{:S(2)}) copy-start(bf16[2304,256]{1,0:T(8,128)(2,1)} %param.23) | copy-start | bytes 3538948
  372.4 211.4 %copy-start.1 = (bf16[576,2304]{1,0:T(8,128)(2,1)S(1)}, bf16[576,2304]{1,0:T(8,128)(2,1)}, u32[]{:S(2)}) copy-start(bf16[576,2304]{1,0:T(8,128)(2,1)} %param.20) | copy-start | bytes 7962628
  386.5 1.4 copy-start.5
  387.8 64.9 %copy-start.8 = (bf16[256,32]{0,1:T(8,128)(2,1)S(1)}, bf16[256,32]{0,1:T(8,128)(2,1)}, u32[]{:S(2)}) copy-start(bf16[256,32]{0,1:T(8,128)(2,1)} %param.26) | copy-start | bytes 49156
  387.8 193.7 %copy-start.6 = (f32[32,32,3,3]{1,0,3,2:T(8,128)S(1)}, f32[32,32,3,3]{1,0,3,2:T(8,128)}, u32[]{:S(2)}) copy-start(f32[32,32,3,3]{1,0,3,2:T(8,128)} %param.27) | copy-start | bytes 110596
  387.8 193.7 %copy-start.11 = (f32[32]{0:T(128)S(1)}, f32[32]{0:T(128)}, u32[]{:S(2)}) copy-start(f32[32]{0:T(128)} %param.28) | copy-start | bytes 388
  387.8 195.4 %copy-start.9 = (f32[1,32,64]{2,1,0:T(8,128)S(1)}, f32[1,32,64]{2,1,0:T(8,128)}, u32[]{:S(2)}) copy-start(f32[1,32,64]{2,1,0:T(8,128)} %param.29) | copy-start | bytes 24580
  388.9 25.6 %collective-permute-start = (f32[1024,256]{0,1:T(8,128)}, f32[1024,256]{0,1:T(8,128)}, u32[]{:S(2)}, u32[]{:S(2)}) collective-permute-start(f32[1024,256]{0,1:T(8,128)} %constant_dynamic-slice_fusion), channel_id=1, source_target_pairs={{0,64},{16,80},{32,96},{48,112},{64,0},{80,16},{96,32},{112,48},{1... | collective-permute-start | bytes 3145736 | tf_op jit(solution)/shard_map/ppermute | solution.py:14
Sparse Core Ops, SparseCore 0:
  10.5 80.0 all-gather.2
  128.2 156.6 reduce-scatter.1
  288.0 75.4 all-gather.4
  455.0 125.3 all-reduce.2
where the time goes:
time: 591 us; the launch traced here: 590 us
  waiting for transfers between devices  405 us (69%)
  blocking collectives  66.8 us (11%)
  other arithmetic  48.6 us (8%)
  matrix products  46.2 us (8%)
  between operations  14 us (2%)
  local copies, waits for them, and re-layouts  9.16 us (2%)
    reduce_scatter x1, waiting for transfers between devices, body(): lax.psum_scatter(jnp.dot(full_hidden, down_weight, preferred_element_type...  156 us
    psum x1, waiting for transfers between devices, body(): lax.psum((mixed_code * factor[:, None]).astype(jnp.bfloat16), 'mp')  92.3 us
    all_gather x1, waiting for transfers between devices, body(): full_out = lax.all_gather(block_out, 'mp', axis=0, tiled=True)  75.9 us
    all_gather x1, waiting for transfers between devices, body(): gathered = lax.all_gather(tokens, 'mp', axis=0, tiled=True)  57.1 us
    pmax x1, blocking collectives, body(): global_peak = lax.pmax(row_peak, 'mp')  33.6 us
    psum x1, blocking collectives, body(): lax.psum((row_total * factor).astype(jnp.bfloat16), 'mp')  33.2 us
    dot_general x1, matrix products, body(): jnp.dot(full_hidden, down_weight, preferred_element_type=jnp.float32)  28.5 us
    select_n x1, other arithmetic, per_image(): picked = jnp.where(chosen, lookup[1], picked)  24.7 us
  transfers between devices with their start and end apart: 5, of which 5 were waited for; matrix products, arithmetic and copies ran while one was open for 5% of the time, Pallas kernels for 0%

commit v1 on v0

--- a/solution.py
+++ b/solution.py
@@ -74,7 +74,10 @@
     block_out = (
         tokens.astype(jnp.float32) + per_image(ffn_gate, own_images) * (summed + down_bias)
     ).astype(jnp.bfloat16)
-    full_out = lax.all_gather(block_out, "mp", axis=0, tiled=True)
+    n_dev = lax.axis_size("mp")
+    pieces = jnp.stack([block_out for _ in range(n_dev)])
+    pieces = lax.all_to_all(pieces, "mp", split_axis=0, concat_axis=0)
+    full_out = jnp.concatenate(pieces, axis=0)
     logits = (
         jnp.dot(
             modulate(full_out.astype(jnp.float32), per_image(ada_head, row_images)),

time: 591 us -> 678 us (1.15)
  waiting for transfers between devices: 405 us -> 464 us
  other arithmetic: 48.6 us -> 67.3 us
  blocking collectives: 66.8 us -> 79.3 us
  matrix products: 46.2 us -> 34.8 us
    all_to_all x0 -> x1, waiting for transfers between devices: none -> 136 us  [body(): pieces = lax.all_to_all(pieces, 'mp', split_axis=0, concat_axis=0)]
    all_gather x1 -> x0, waiting for transfers between devices: 75.9 us -> none  [body(): full_out = lax.all_gather(block_out, 'mp', axis=0, tiled=True)]
    convert_element_type x0 -> x1, other arithmetic: none -> 15.9 us  [modulate(): (norm_rows(values) * (1.0 + ada_rows[:, 1]) + ada_rows[:, 0]).astype(jnp....]
    pmax x1, blocking collectives: 33.6 us -> 46.1 us  [body(): global_peak = lax.pmax(row_peak, 'mp')]
    dot_general x1, matrix products: 14 us -> 2.66 us  [body(): jnp.dot(modulate(full_out.astype(jnp.float32), per_image(ada_head, row_im...]
  transfers between devices with their start and end apart: 5 -> 5, of which waited for: 5 -> 5; matrix products, arithmetic and copies ran while one was open for 5% -> 4% of each run, Pallas kernels for 0% -> 0%
where the time goes in v1:
time: 678 us; the launch traced here: 677 us
  waiting for transfers between devices  464 us (68%)
  blocking collectives  79.3 us (12%)
  other arithmetic  67.3 us (10%)
  matrix products  34.8 us (5%)
  between operations  14.1 us (2%)
  local copies, waits for them, and re-layouts  12.4 us (2%)
    reduce_scatter x1, waiting for transfers between devices, body(): lax.psum_scatter(jnp.dot(full_hidden, down_weight, preferred_element_type...  156 us
    all_to_all x1, waiting for transfers between devices, body(): pieces = lax.all_to_all(pieces, 'mp', split_axis=0, concat_axis=0)  136 us
    psum x1, waiting for transfers between devices, body(): lax.psum((mixed_code * factor[:, None]).astype(jnp.bfloat16), 'mp')  92.3 us
    all_gather x1, waiting for transfers between devices, body(): gathered = lax.all_gather(tokens, 'mp', axis=0, tiled=True)  57.1 us
    pmax x1, blocking collectives, body(): global_peak = lax.pmax(row_peak, 'mp')  46.1 us
    psum x1, blocking collectives, body(): lax.psum((row_total * factor).astype(jnp.bfloat16), 'mp')  33.2 us
    dot_general x1, matrix products, body(): jnp.dot(full_hidden, down_weight, preferred_element_type=jnp.float32)  28.5 us
    select_n x1, other arithmetic, per_image(): picked = jnp.where(chosen, lookup[1], picked)  24.7 us
  transfers between devices with their start and end apart: 5, of which 5 were waited for; matrix products, arithmetic and copies ran while one was open for 4% of the time, Pallas kernels for 0%

profile of v1, /device:TPU:0, one launch (start us, length us, event | category | flops | bytes accessed | tf_op | source)
XLA Modules:
  0.0 677.2 jit_solution(7137891148437685837)
XLA Ops:
  8.8 24.7 %broadcast_select_fusion = (f32[2048,2,2304]{2,0,1:T(8,128)}, f32[2048,2,2304]{2,0,1:T(8,128)}) fusion(f32[2,2304]{1,0:T(2,128)S(1)} %get-tuple-element.9, f32[2,2304]{1,0:T(2,128)S(1)} %get-tuple-element.8, pred[2048]{0:T(1024)(128)(4,1)S(1)} %fusion.63, f32[2,2304]{1,0:T(2,128)S(1)} %get-tuple-element.16, f32[2,2304]{1,0:T(2,128)S(1)} %get-tuple-element.17), kind=kLoop, calls=%fused_computation.19 | loop fusion | flops 18874368 | bytes 75573248 | tf_op jit(solution)/shard_map/jit(_where)/select_n | solution.py:27
  33.4 57.1 %all-gather.2.cloned.1.call-done = bf16[2048,2304]{1,0:T(8,128)(2,1)} async-done(((bf16[128,2304]{1,0:T(8,128)(2,1)}), bf16[2048,2304]{1,0:T(8,128)(2,1)}) %all-gather.2.cloned.1.call-update) | async-done | bytes 9437200 | tf_op jit(solution)/shard_map/all_gather | solution.py:57
  90.6 5.1 convert_reduce_fusion
  95.7 1.2 copy-done.2
  96.9 2.6 fusion.2
  99.6 28.5 %fusion.25 = f32[2048,2304]{1,0:T(8,128)} fusion(bf16[576,2304]{1,0:T(8,128)(2,1)S(1)} %copy-done, bf16[2304,576]{0,1:T(8,128)(2,1)} %param.18, bf16[2048,2304]{1,0:T(8,128)(2,1)} %all-gather.2.cloned.1.call-done, f32[2048,2,2304]{2,0,1:T(8,128)} %get-tuple-element.15, f32[2048]{0:T(1024)S(1)} %add_rsqrt_fusion, f32[2048]{0:T(1024)S(1)} %broadcast_multiply_fusion.1, ...), kind=kOutput, calls=%fused_computation.33 | convolution fusion | flops 10916462592 | bytes 71387392 | tf_op jit(solution)/shard_map/dot_general | solution.py:69
  128.9 156.1 %reduce-scatter.2.cloned.1.call-done = f32[128,2304]{1,0:T(8,128)} async-done(((f32[2048,2304]{1,0:T(8,128)}), f32[128,2304]{1,0:T(8,128)}) %reduce-scatter.2.cloned.1.call-update) | async-done | bytes 1179664 | tf_op jit(solution)/shard_map/reduce_scatter | solution.py:68
  285.0 1.5 add_convert_fusion
  286.5 4.4 stack.2
  290.9 4.8 all-to-all-start
  296.0 135.7 %all-to-all-done = bf16[16,128,2304]{2,1,0:T(8,128)(2,1)} async-done(((bf16[16,128,2304]{2,1,0:T(8,128)(2,1)}), bf16[16,128,2304]{2,1,0:T(8,128)(2,1)}, u32[]{:S(2)}, u32[]{:S(2)}) %all-to-all-start) | async-done | bytes 9437216 | tf_op jit(solution)/shard_map/all_to_all | solution.py:79
  431.7 5.0 convert_reduce_fusion.1
  436.6 6.3 multiply_reduce_fusion
  443.0 15.9 %fusion.7 = bf16[2048,2304]{1,0:T(8,128)(2,1)S(1)} fusion(f32[2048,2,2304]{2,0,1:T(8,128)} %get-tuple-element.14, bf16[16,128,2304]{2,1,0:T(8,128)(2,1)} %all-to-all-done, f32[2048]{0:T(1024)S(1)} %rsqrt_bitcast_fusion, f32[2048]{0:T(1024)S(1)} %get-tuple-element.12), kind=kLoop, calls=%fused_computation.10 | loop fusion | flops 33030144 | bytes 56639488 | tf_op jit(solution)/shard_map/convert_element_type | solution.py:32
  458.9 2.7 convolution_add_fusion
  461.6 1.3 copy-done.5
  464.0 2.5 copy.17
  466.6 22.3 %collective-permute-done = f32[1024,256]{0,1:T(8,128)} collective-permute-done((f32[1024,256]{0,1:T(8,128)}, f32[1024,256]{0,1:T(8,128)}, u32[]{:S(2)}, u32[]{:S(2)}) %collective-permute-start) | collective-permute-done | bytes 1048608 | tf_op jit(solution)/shard_map/ppermute | solution.py:14
  488.8 3.3 fusion.90
  492.1 46.1 %pmax.7 = f32[1024]{0:T(1024)S(1)} all-reduce(f32[1024]{0:T(1024)S(1)} %get-tuple-element.6), channel_id=1, replica_groups=mesh['dp'=8,'mp'=16] {'mp'}, use_global_device_ids=true, to_apply=%region_6.7 | all-reduce | flops 1024 | bytes 8192 | tf_op jit(solution)/shard_map/pmax | solution.py:101
  538.2 1.4 convert_reduce_fusion.2
  539.6 2.1 fusion.32
  541.7 33.2 %psum.15 = bf16[1024]{0:T(1024)(128)(2,1)S(1)} all-reduce(bf16[1024]{0:T(1024)(128)(2,1)S(1)} %get-tuple-element.4), channel_id=1, replica_groups=mesh['dp'=8,'mp'=16] {'mp'}, use_global_device_ids=true, to_apply=%region_9.10 | all-reduce | flops 1024 | bytes 4096 | tf_op jit(solution)/shard_map/psum | solution.py:104
  574.9 92.3 %all-reduce.3.cloned.1.call-done = bf16[1024,32]{0,1:T(8,128)(2,1)} async-done(((bf16[1024,32]{0,1:T(8,128)(2,1)}), bf16[1024,32]{0,1:T(8,128)(2,1)}) %all-reduce.3.cloned.1.call-update) | async-done | bytes 65552 | tf_op jit(solution)/shard_map/psum | solution.py:105
  (59 shorter events, 7.0 us)
Async XLA Ops:
  7.2 92.4 %copy-start = (bf16[576,2304]{1,0:T(8,128)(2,1)S(1)}, bf16[576,2304]{1,0:T(8,128)(2,1)}, u32[]{:S(2)}) copy-start(bf16[576,2304]{1,0:T(8,128)(2,1)} %param.20) | copy-start | bytes 7962628
  7.2 83.4 %all-gather.2.cloned.1.call-start = ((), (), s32[]{:S(2)}) async-start(), calls=%async_computation.2 | async-start | bytes 10027008 | tf_op jit(solution)/shard_map/all_gather | solution.py:57
  7.9 277.0 %reduce-scatter.2.cloned.1.call-start = ((), (), s32[]{:S(2)}) async-start(), calls=%async_computation.3 | async-start | bytes 20054016 | tf_op jit(solution)/shard_map/reduce_scatter | solution.py:68
  33.4 66.1 %copy-start.13 = (f32[576]{0:T(1024)S(1)}, f32[576]{0:T(1024)}, u32[]{:S(2)}) copy-start(f32[576]{0:T(1024)} %param.19) | copy-start | bytes 6916
  90.6 6.4 copy-start.2
  128.1 0.7 copy-start.7
  128.1 156.9 %copy-start.4 = (bf16[128,2304]{1,0:T(8,128)(2,1)S(1)}, bf16[128,2304]{1,0:T(8,128)(2,1)}, u32[]{:S(2)}) copy-start(bf16[128,2304]{1,0:T(8,128)(2,1)} %param.15) | copy-start | bytes 1769476
  128.1 156.9 %copy-start.10 = (f32[2304]{0:T(1024)S(1)}, f32[2304]{0:T(1024)}, u32[]{:S(2)}) copy-start(f32[2304]{0:T(1024)} %param.21) | copy-start | bytes 27652
  286.5 4.4 copy-start.3
  290.9 140.7 %all-to-all-start = ((bf16[16,128,2304]{2,1,0:T(8,128)(2,1)}), bf16[16,128,2304]{2,1,0:T(8,128)(2,1)}, u32[]{:S(2)}, u32[]{:S(2)}) async-start(bf16[16,128,2304]{2,1,0:T(8,128)(2,1)} %stack.2), calls=%async_computation.1 | async-start | bytes 18874368 | tf_op jit(solution)/shard_map/all_to_all | solution.py:79
  295.7 371.5 %all-reduce.3.cloned.1.call-start = ((), (), s32[]{:S(2)}) async-start(), calls=%async_computation.4 | async-start | bytes 131072 | tf_op jit(solution)/shard_map/psum | solution.py:105
  442.9 16.0 %copy-start.12 = (bf16[2304,256]{1,0:T(8,128)(2,1)S(1)}, bf16[2304,256]{1,0:T(8,128)(2,1)}, u32[]{:S(2)}) copy-start(bf16[2304,256]{1,0:T(8,128)(2,1)} %param.23) | copy-start | bytes 3538948
  442.9 16.0 %copy-start.14 = (f32[256]{0:T(256)S(1)}, f32[256]{0:T(256)}, u32[]{:S(2)}) copy-start(f32[256]{0:T(256)} %param.24) | copy-start | bytes 3076
  458.9 211.8 %copy-start.1 = (bf16[576,2304]{1,0:T(8,128)(2,1)S(1)}, bf16[576,2304]{1,0:T(8,128)(2,1)}, u32[]{:S(2)}) copy-start(bf16[576,2304]{1,0:T(8,128)(2,1)} %param.20) | copy-start | bytes 7962628
  461.6 1.4 copy-start.5
  462.9 76.6 %copy-start.8 = (bf16[256,32]{0,1:T(8,128)(2,1)S(1)}, bf16[256,32]{0,1:T(8,128)(2,1)}, u32[]{:S(2)}) copy-start(bf16[256,32]{0,1:T(8,128)(2,1)} %param.26) | copy-start | bytes 49156
  462.9 205.4 %copy-start.6 = (f32[32,32,3,3]{1,0,3,2:T(8,128)S(1)}, f32[32,32,3,3]{1,0,3,2:T(8,128)}, u32[]{:S(2)}) copy-start(f32[32,32,3,3]{1,0,3,2:T(8,128)} %param.27) | copy-start | bytes 110596
  462.9 205.4 %copy-start.11 = (f32[32]{0:T(128)S(1)}, f32[32]{0:T(128)}, u32[]{:S(2)}) copy-start(f32[32]{0:T(128)} %param.28) | copy-start | bytes 388
  462.9 207.1 %copy-start.9 = (f32[1,32,64]{2,1,0:T(8,128)S(1)}, f32[1,32,64]{2,1,0:T(8,128)}, u32[]{:S(2)}) copy-start(f32[1,32,64]{2,1,0:T(8,128)} %param.29) | copy-start | bytes 24580
  464.0 24.8 %collective-permute-start = (f32[1024,256]{0,1:T(8,128)}, f32[1024,256]{0,1:T(8,128)}, u32[]{:S(2)}, u32[]{:S(2)}) collective-permute-start(f32[1024,256]{0,1:T(8,128)} %constant_dynamic-slice_fusion), channel_id=1, source_target_pairs={{0,64},{16,80},{32,96},{48,112},{64,0},{80,16},{96,32},{112,48},{1... | collective-permute-start | bytes 3145736 | tf_op jit(solution)/shard_map/ppermute | solution.py:14
Sparse Core Ops, SparseCore 0:
  10.5 80.0 all-gather.1
  128.2 156.6 reduce-scatter.1
  541.8 125.3 all-reduce.2
